TPU v7x, 32 devices: a whole 2x2x4 slice. The times are simulated.
32 devices in a mesh: dp: 8 (over y, x, core), ctx: 4 (over z).
Axes of the slice: x: 2, y: 2, z: 4, core: 2. Of those that a mesh axis runs over, the one named last changes fastest.
Arguments:
- inputs: bfloat16 [8, 1024, 2048], P('dp', 'ctx'), may hold values from -6 to 6
- lengths: int32 [8], P('dp'), may hold values from 512 to 1024, as said below
- norm_gain: bfloat16 [2048], replicated, may hold values from 0.5 to 1.5
- up_weight: bfloat16 [2048, 8192], P('dp'), may hold values from -0.125 to 0.125
- conv_weight: bfloat16 [4, 4096], replicated, may hold values from -3 to 3
- conv_bias: bfloat16 [4096], replicated, may hold values from -3 to 3
- qkv_weight: bfloat16 [3, 4, 4, 4, 256], replicated, may hold values from -3 to 3
- gate_weight: bfloat16 [8, 12288], replicated, may hold values from -0.109375 to 0.109375
- gate_bias: bfloat16 [8], replicated, may hold values from -1 to 8.5
- skip_weight: bfloat16 [4096], replicated, may hold values from 0.5 to 1.5
- outnorm_weight: bfloat16 [4096], replicated, may hold values from 0.5 to 1.5
- down_weight: bfloat16 [4096, 2048], P('dp'), may hold values from -0.09375 to 0.09375
- grad_out: bfloat16 [8, 1024, 2048], P('dp', 'ctx'), may hold values from -6 to 6
Outputs:
- outputs: bfloat16 [8, 1024, 2048], P('dp', 'ctx')
- grad_inputs: float32 [8, 1024, 2048], P('dp', 'ctx')
- grad_norm_gain: float32 [2048], replicated
- grad_up_weight: float32 [2048, 8192], P('dp')
- grad_conv_weight: float32 [4, 4096], replicated
- grad_conv_bias: float32 [4096], replicated
- grad_qkv_weight: float32 [3, 4, 4, 4, 256], replicated
- grad_gate_weight: float32 [8, 12288], replicated
- grad_gate_bias: float32 [8], replicated
- grad_skip_weight: float32 [4096], replicated
- grad_outnorm_weight: float32 [4096], replicated
- grad_down_weight: float32 [4096, 2048], P('dp')
Inputs may be any that keep to these rules, and one draw needn't show every extreme that they name: `lengths`: each entry counts the real tokens of a sequence from its start; one sequence has exactly 1024, another exactly 512.
All inputs are finite; a program needn't handle non-finite values.
Results may differ from a plain program's by a relative error of at most 0.04.
Values may be sent and summed in bfloat16 or wider, within the bound.
No kernel may reach another device: no remote copies, remote signals or barrier semaphores. Data moves between devices by JAX's collectives and lax.ppermute only.
A program may use at most 448 MiB of HBM per device.

v0:
```python
from functools import partial
import jax
import jax.numpy as jnp
from jax import lax
from jax.sharding import PartitionSpec as P

highest = lax.Precision.HIGHEST
epsilon = 1e-05


def shifted(x, axis, by):
    length = lax.axis_size(axis)
    pairs = [(i, i + by) for i in range(length) if 0 <= i + by < length]
    return lax.ppermute(x, axis, pairs)


def low(value_in):
    rounded = lax.optimization_barrier(value_in.astype(jnp.bfloat16)).astype(jnp.float32)
    return value_in + lax.stop_gradient(rounded - value_in)


def layer_norm_low(rows_in, gain_row):
    centred = rows_in - jnp.mean(rows_in, axis=-1, keepdims=True)
    spread = jnp.mean(centred * centred, axis=-1, keepdims=True)
    return low(centred * lax.rsqrt(spread + epsilon) * gain_row)


def headwise(values_in, blocks_in):
    row_count, width_all = values_in.shape
    head_count, block_size, block_out, block_count = blocks_in.shape
    grouped = values_in.reshape(row_count, head_count, block_size, block_count)
    mixed_rows = jnp.einsum("thij,hioj->thoj", grouped, blocks_in, precision=highest)
    return mixed_rows.reshape(row_count, width_all)


def split_heads(rows_in, head_count):
    return rows_in.reshape(rows_in.shape[0], head_count, -1).transpose(1, 0, 2)


def mid_section(mixer_in, rim_rows, conv_taps, conv_shift, qkv_blocks, gate_matrix, gate_offset):
    row_count, width_all = mixer_in.shape
    kernel_size = conv_taps.shape[0]
    head_count = qkv_blocks.shape[1]
    padded_in = jnp.concatenate([rim_rows, mixer_in], axis=0)
    conv_pre = conv_shift[None, :] + conv_taps[0][None, :] * padded_in[0:row_count]
    for tap_index in range(1, kernel_size):
        conv_pre = (
            conv_pre + conv_taps[tap_index][None, :] * padded_in[tap_index : tap_index + row_count]
        )
    conv_out = jax.nn.silu(conv_pre)
    key_scale = (width_all // head_count) ** (-0.5)
    queries = low(headwise(conv_out, qkv_blocks[0]))
    key_rows = low(headwise(conv_out, qkv_blocks[1]) * key_scale)
    value_rows = low(headwise(mixer_in, qkv_blocks[2]))
    joined = jnp.concatenate([queries, key_rows, value_rows], axis=1)
    gate_pre = jnp.dot(joined, gate_matrix.T, precision=highest) + gate_offset[None, :]
    return (
        queries,
        key_rows,
        value_rows,
        gate_pre[:, :head_count],
        jax.nn.log_sigmoid(gate_pre[:, head_count:]),
        conv_out,
    )


def cell_scores(queries, key_rows, head_count):
    return jnp.einsum(
        "htk,hsk->hts",
        split_heads(queries, head_count),
        split_heads(key_rows, head_count),
        precision=highest,
    )


def cell_rest(scores, queries, value_rows, in_gate, log_forget, state_in):
    row_count, width_all = queries.shape
    head_count = state_in.shape[0]
    query_heads = split_heads(queries, head_count)
    value_heads = split_heads(value_rows, head_count)
    decay_sum = jnp.cumsum(log_forget, axis=0).T
    gate_row = in_gate.T
    causal = jnp.arange(row_count)[:, None] >= jnp.arange(row_count)[None, :]
    exponent = decay_sum[:, :, None] - decay_sum[:, None, :] + gate_row[:, None, :]
    weights = jnp.where(causal[None], jnp.exp(jnp.where(causal[None], exponent, 0.0)), 0.0)
    mix_weights = low(weights * scores)
    within = jnp.einsum("hts,hsd->htd", mix_weights, value_heads, precision=highest)
    carried = jnp.einsum("htk,hkd->htd", query_heads, low(state_in), precision=highest)
    numerator = within + jnp.exp(decay_sum)[:, :, None] * carried
    return numerator.transpose(1, 0, 2).reshape(row_count, width_all)


def summary(key_rows, value_rows, in_gate, log_forget):
    head_count = in_gate.shape[1]
    decay_sum = jnp.cumsum(log_forget, axis=0)
    span_decay = decay_sum[-1]
    weights = jnp.exp(span_decay[None, :] - decay_sum + in_gate)
    weighted = low(split_heads(key_rows, head_count) * weights.T[:, :, None])
    state_part = jnp.einsum(
        "htk,htd->hkd", weighted, split_heads(value_rows, head_count), precision=highest
    )
    return (state_part, span_decay)


def tail_section(numerator, conv_out, gate_in, outnorm_scale, skip_scale, head_count):
    row_count, width_all = numerator.shape
    grouped = numerator.reshape(row_count, head_count, -1)
    centred = grouped - jnp.mean(grouped, axis=-1, keepdims=True)
    spread = jnp.mean(centred * centred, axis=-1, keepdims=True)
    normed = (centred * lax.rsqrt(spread + epsilon)).reshape(row_count, width_all) * outnorm_scale
    return low((normed + skip_scale * conv_out) * jax.nn.silu(gate_in))


def on_device(
    inputs,
    lengths,
    norm_gain,
    up_weight,
    conv_weight,
    conv_bias,
    qkv_weight,
    gate_weight,
    gate_bias,
    skip_weight,
    outnorm_weight,
    down_weight,
    grad_out,
):
    span_len = inputs.shape[1]
    inner_width = conv_weight.shape[1]
    head_count = qkv_weight.shape[1]
    kernel_size = conv_weight.shape[0]
    ctx_count = lax.axis_size("ctx")
    ctx_index = lax.axis_index("ctx")
    positions = ctx_index * span_len + jnp.arange(span_len)
    live_rows = (positions < lengths[0]).astype(jnp.float32)[:, None]
    rows_in = inputs[0].astype(jnp.float32)
    norm_scale = norm_gain.astype(jnp.float32)
    conv_taps = conv_weight.astype(jnp.float32)
    conv_shift = conv_bias.astype(jnp.float32)
    qkv_blocks = qkv_weight.astype(jnp.float32)
    gate_matrix = gate_weight.astype(jnp.float32)
    gate_offset = gate_bias.astype(jnp.float32)
    skip_scale = skip_weight.astype(jnp.float32)
    outnorm_scale = outnorm_weight.astype(jnp.float32)
    contract_last = (((1,), (1,)), ((), ()))
    contract_first = (((0,), (0,)), ((), ()))
    normed, front_back = jax.vjp(layer_norm_low, rows_in, norm_scale)
    normed_low = normed.astype(jnp.bfloat16)
    columns = normed_low
    upward = jnp.dot(
        columns,
        lax.all_gather(up_weight, "dp", axis=0, tiled=True),
        preferred_element_type=jnp.float32,
    )
    mixer_low = upward[:, :inner_width].astype(jnp.bfloat16)
    mixer_in = mixer_low.astype(jnp.float32)
    gate_in = upward[:, inner_width:]
    rim_rows = shifted(mixer_low[span_len - kernel_size + 1 :], "ctx", 1).astype(jnp.float32)
    mid_result, mid_back = jax.vjp(
        mid_section, mixer_in, rim_rows, conv_taps, conv_shift, qkv_blocks, gate_matrix, gate_offset
    )
    queries, key_rows, value_rows, in_gate, log_forget, conv_out = mid_result
    summed, summary_back = jax.vjp(summary, key_rows, value_rows, in_gate, log_forget)
    state_part, span_decay = summed

    def relay(turn, carried):
        return shifted(jnp.exp(span_decay)[:, None, None] * carried + state_part, "ctx", 1)

    state_in = lax.fori_loop(0, ctx_count - 1, relay, jnp.zeros_like(state_part))
    scores, score_back = jax.vjp(partial(cell_scores, head_count=head_count), queries, key_rows)
    numerator, rest_back = jax.vjp(
        cell_rest, scores, queries, value_rows, in_gate, log_forget, state_in
    )
    hidden_state, tail_back = jax.vjp(
        partial(tail_section, head_count=head_count),
        numerator,
        conv_out,
        gate_in,
        outnorm_scale,
        skip_scale,
    )
    hidden_low = hidden_state.astype(jnp.bfloat16)
    columns = hidden_low
    branch = jnp.dot(
        columns,
        lax.all_gather(down_weight, "dp", axis=0, tiled=True),
        preferred_element_type=jnp.float32,
    )
    outputs = (live_rows * (rows_in + branch)).astype(jnp.bfloat16)[None]
    out_grad = grad_out[0].astype(jnp.float32) * live_rows
    branch_grad = out_grad.astype(jnp.bfloat16)
    hidden_grad = lax.dot_general(
        branch_grad,
        lax.all_gather(down_weight, "dp", axis=0, tiled=True),
        contract_last,
        preferred_element_type=jnp.float32,
    )
    numer_raw, conv_tail_grad, gate_in_grad, outnorm_grad, skip_grad = tail_back(hidden_grad)
    numer_low = numer_raw.astype(jnp.bfloat16)
    numer_grad = numer_low.astype(jnp.float32)
    scores_raw, query_part, value_grad, ingate_grad, forget_grad, state_grad = rest_back(numer_grad)
    query_extra, key_grad = score_back(scores_raw.astype(jnp.bfloat16).astype(jnp.float32))
    query_grad = query_part + query_extra

    def relay_back(turn, carried):
        return shifted(jnp.exp(span_decay)[:, None, None] * carried + state_grad, "ctx", -1)

    later_grad = lax.fori_loop(0, ctx_count - 1, relay_back, jnp.zeros_like(state_grad))
    decay_grad = jnp.exp(span_decay) * jnp.sum(later_grad * state_in, axis=(1, 2))
    later_rounded = later_grad.astype(jnp.bfloat16).astype(jnp.float32)
    key_extra, value_extra, ingate_extra, forget_extra = summary_back((later_rounded, decay_grad))
    mid_grads = mid_back(
        (
            query_grad,
            key_grad + key_extra,
            value_grad + value_extra,
            ingate_grad + ingate_extra,
            forget_grad + forget_extra,
            conv_tail_grad,
        )
    )
    (
        mixer_grad,
        rim_grad,
        conv_taps_grad,
        conv_shift_grad,
        qkv_grad,
        gate_matrix_grad,
        gate_offset_grad,
    ) = mid_grads
    rim_returned = shifted(rim_grad.astype(jnp.bfloat16), "ctx", -1).astype(rim_grad.dtype)
    mixer_grad = mixer_grad + jnp.pad(rim_returned, ((span_len - kernel_size + 1, 0), (0, 0)))
    upward_grad = jnp.concatenate([mixer_grad, gate_in_grad], axis=1).astype(jnp.bfloat16)
    normed_grad = lax.dot_general(
        upward_grad,
        lax.all_gather(up_weight, "dp", axis=0, tiled=True),
        contract_last,
        preferred_element_type=jnp.float32,
    )
    front_grad, norm_scale_grad = front_back(normed_grad)
    input_grad = (out_grad + front_grad)[None]
    columns = normed_low
    up_part = lax.psum_scatter(
        lax.dot_general(
            columns, upward_grad, contract_first, preferred_element_type=jnp.float32
        ).astype(jnp.bfloat16),
        "dp",
        scatter_dimension=0,
        tiled=True,
    )
    columns = hidden_low
    down_part = lax.psum_scatter(
        lax.dot_general(
            columns, branch_grad, contract_first, preferred_element_type=jnp.float32
        ).astype(jnp.bfloat16),
        "dp",
        scatter_dimension=0,
        tiled=True,
    )
    up_total, down_total = (
        lax.psum(up_part, "ctx").astype(jnp.float32),
        lax.psum(down_part, "ctx").astype(jnp.float32),
    )
    small_total = lax.psum(
        (
            norm_scale_grad,
            conv_taps_grad,
            conv_shift_grad,
            qkv_grad,
            gate_matrix_grad,
            gate_offset_grad,
            skip_grad,
            outnorm_grad,
        ),
        ("dp", "ctx"),
    )
    return (
        outputs,
        input_grad,
        small_total[0],
        up_total,
        small_total[1],
        small_total[2],
        small_total[3],
        small_total[4],
        small_total[5],
        small_total[6],
        small_total[7],
        down_total,
    )


def solution(mesh):
    return jax.shard_map(
        on_device,
        mesh=mesh,
        in_specs=(
            P("dp", "ctx", None),
            P("dp"),
            P(),
            P("dp", None),
            P(),
            P(),
            P(),
            P(),
            P(),
            P(),
            P(),
            P("dp", None),
            P("dp", "ctx", None),
        ),
        out_specs=(
            P("dp", "ctx", None),
            P("dp", "ctx", None),
            P(),
            P("dp", None),
            P(),
            P(),
            P(),
            P(),
            P(),
            P(),
            P(),
            P("dp", None),
        ),
        check_vma=False,
    )
```

profile of v0, /device:TPU:0, one launch (start us, length us, event | category | flops | bytes accessed | tf_op | source)
XLA Modules:
  0.0 3726.6 jit_solution(15394948117392416776)
XLA Ops:
  16.5 157.0 %all-gather.3.cloned.1.call-done = bf16[2048,8192]{1,0:T(8,128)(2,1)} async-done(((bf16[256,8192]{1,0:T(8,128)(2,1)}), bf16[2048,8192]{1,0:T(8,128)(2,1)}) %all-gather.3.cloned.1.call-update) | async-done | bytes 33554448 | tf_op jit(solution)/shard_map/all_gather | solution.py:153
  173.5 19.8 fusion.142
  214.1 51.2 %all-gather.5.cloned.1.call-done = bf16[4096,2048]{1,0:T(8,128)(2,1)} async-done(((bf16[512,2048]{1,0:T(8,128)(2,1)}), bf16[4096,2048]{1,0:T(8,128)(2,1)}) %all-gather.5.cloned.1.call-update) | async-done | bytes 16777232 | tf_op jit(solution)/shard_map/all_gather | solution.py:187
  265.3 12.3 broadcast_multiply_fusion
  344.5 10.2 fusion.100
  357.9 29.3 fusion.54
  387.1 8.0 broadcast.160.clone
  395.1 1142.1 %while.24 = (s32[]{:T(128)}, f32[4,1024,1024]{2,1,0:T(8,128)}, f32[4,1,1]{0,2,1:T(1,128)S(1)}, f32[4,1024,1024]{2,1,0:T(8,128)}, s32[]{:T(128)}) while((s32[]{:T(128)}, f32[4,1024,1024]{2,1,0:T(8,128)}, f32[4,1,1]{0,2,1:T(1,128)S(1)}, f32[4,1024,1024]{2,1,0:T(8,128)}, s32[]{:T(128)}) %tuple.133), condition=%wide.region_5.6_spmd, body=%wide.region_4.5_spmd.sunk | while | flops 8388610 | bytes 117440624 | solution.py:170
  395.1 17.3 multiply_add_fusion.10
  412.4 9.2 collective-permute-start
  421.7 354.4 %collective-permute-done = f32[4,1024,1024]{2,1,0:T(8,128)} collective-permute-done((f32[4,1024,1024]{2,1,0:T(8,128)}, f32[4,1024,1024]{2,1,0:T(8,128)}, u32[]{:S(2)}, u32[]{:S(2)}) %collective-permute-start) | collective-permute-done | bytes 16777248 | tf_op jit(solution)/shard_map/while/body/eval_jaxpr/ppermute | solution.py:14
  776.0 17.3 multiply_add_fusion.10
  793.3 10.2 collective-permute-start
  803.6 353.6 %collective-permute-done = f32[4,1024,1024]{2,1,0:T(8,128)} collective-permute-done((f32[4,1024,1024]{2,1,0:T(8,128)}, f32[4,1024,1024]{2,1,0:T(8,128)}, u32[]{:S(2)}, u32[]{:S(2)}) %collective-permute-start) | collective-permute-done | bytes 16777248 | tf_op jit(solution)/shard_map/while/body/eval_jaxpr/ppermute | solution.py:14
  1157.1 17.3 multiply_add_fusion.10
  1174.4 10.2 collective-permute-start
  1184.6 352.6 %collective-permute-done = f32[4,1024,1024]{2,1,0:T(8,128)} collective-permute-done((f32[4,1024,1024]{2,1,0:T(8,128)}, f32[4,1024,1024]{2,1,0:T(8,128)}, u32[]{:S(2)}, u32[]{:S(2)}) %collective-permute-start) | collective-permute-done | bytes 16777248 | tf_op jit(solution)/shard_map/while/body/eval_jaxpr/ppermute | solution.py:14
  1537.3 9.3 convert_element_type.160
  1547.3 22.0 fusion.1
  1569.3 12.2 fusion.143
  1591.8 21.5 fusion
  1613.3 18.2 fusion.4
  1639.4 1136.2 %while.25 = (s32[]{:T(128)}, f32[4,1024,1024]{2,1,0:T(8,128)}, f32[4,1,1]{0,2,1:T(1,128)S(1)}, f32[4,1024,1024]{2,1,0:T(8,128)}, s32[]{:T(128)}) while((s32[]{:T(128)}, f32[4,1024,1024]{2,1,0:T(8,128)}, f32[4,1,1]{0,2,1:T(1,128)S(1)}, f32[4,1024,1024]{2,1,0:T(8,128)}, s32[]{:T(128)}) %tuple.134), condition=%wide.region_11.12_spmd, body=%wide.region_10.11_spmd.sunk | while | flops 8388610 | bytes 117440624 | solution.py:209
  1639.4 17.3 multiply_add_fusion.11
  1658.0 361.4 %collective-permute-done.1 = f32[4,1024,1024]{2,1,0:T(8,128)} collective-permute-done((f32[4,1024,1024]{2,1,0:T(8,128)}, f32[4,1024,1024]{2,1,0:T(8,128)}, u32[]{:S(2)}, u32[]{:S(2)}) %collective-permute-start.1) | collective-permute-done | bytes 16777248 | tf_op jit(solution)/shard_map/while/body/eval_jaxpr/ppermute | solution.py:14
  2019.4 17.3 multiply_add_fusion.11
  2038.0 360.0 %collective-permute-done.1 = f32[4,1024,1024]{2,1,0:T(8,128)} collective-permute-done((f32[4,1024,1024]{2,1,0:T(8,128)}, f32[4,1024,1024]{2,1,0:T(8,128)}, u32[]{:S(2)}, u32[]{:S(2)}) %collective-permute-start.1) | collective-permute-done | bytes 16777248 | tf_op jit(solution)/shard_map/while/body/eval_jaxpr/ppermute | solution.py:14
  2398.0 17.3 multiply_add_fusion.11
  2416.6 359.1 %collective-permute-done.1 = f32[4,1024,1024]{2,1,0:T(8,128)} collective-permute-done((f32[4,1024,1024]{2,1,0:T(8,128)}, f32[4,1024,1024]{2,1,0:T(8,128)}, u32[]{:S(2)}, u32[]{:S(2)}) %collective-permute-start.1) | collective-permute-done | bytes 16777248 | tf_op jit(solution)/shard_map/while/body/eval_jaxpr/ppermute | solution.py:14
  2775.7 12.8 multiply_reduce_fusion
  2788.5 14.3 fusion.39
  2802.9 18.8 fusion.36
  2902.4 7.9 fusion.63
  2936.7 8.3 fusion.66
  2958.3 20.6 multiply_reduce_fusion.1
  2978.9 11.3 convolution_convert_fusion.1
  3004.2 10.0 broadcast_multiply_fusion.1
  3052.4 17.5 convolution_convert_fusion
  3071.5 8.2 fusion.81
  3079.7 9.0 fusion.84
  3088.7 9.7 fusion.87
  3106.8 11.2 fusion.2
  3119.0 194.8 %reduce-scatter.3.cloned.1.call-done = bf16[256,8192]{1,0:T(8,128)(2,1)} async-done(((bf16[2048,8192]{1,0:T(8,128)(2,1)}), bf16[256,8192]{1,0:T(8,128)(2,1)}) %reduce-scatter.3.cloned.1.call-update) | async-done | bytes 4194320 | tf_op jit(solution)/shard_map/reduce_scatter | solution.py:244
  3314.0 12.7 fusion.53
  3326.7 15.3 fusion.71
  3342.9 41.4 %all-reduce.15 = (f32[2048]{0:T(1024)}, f32[4096]{0:T(1024)}, f32[8]{0:T(128)}, f32[4096]{0:T(1024)}, f32[4096]{0:T(1024)}) all-reduce(f32[2048]{0:T(1024)S(1)} %get-tuple-element.147, f32[4096]{0:T(1024)S(1)} %get-tuple-element.193, f32[8]{0:T(128)S(1)} %fusion.106, ...), channel_id=1, replica_groups=mesh['dp'=8,'ctx'=4] {'dp','ctx'}, use_global_device_ids=true, to_apply=%region_25.26 | all-reduce | flops 14344 | bytes 114752 | tf_op jit(solution)/shard_map/psum | solution.py:265
  3387.7 95.7 %all-reduce.21.cloned.1.call-done = (f32[4,4096]{1,0:T(4,128)}, f32[3,4,4,4,256]{2,3,4,1,0:T(4,128)}, f32[8,12288]{1,0:T(8,128)}) async-done(((f32[4,4096]{1,0:T(4,128)}, f32[3,4,4,4,256]{2,3,4,1,0:T(4,128)}, f32[8,12288]{1,0:T(8,128)}), (f32[4,4096]{1,0:T(4,128)}, f32[3,4,4,4,256]{2,3,4,1,0:T(4,128)}, f32[8,12288]{1,0:T(8,128)})) %all-reduce.21.cloned.1.call-update) | async-done | bytes 655376 | tf_op jit(solution)/shard_map/psum | solution.py:265
  3489.5 219.5 %all-reduce.23.cloned.1.call-done = (bf16[256,8192]{1,0:T(8,128)(2,1)}, bf16[512,2048]{1,0:T(8,128)(2,1)}) async-done(((bf16[256,8192]{1,0:T(8,128)(2,1)}, bf16[512,2048]{1,0:T(8,128)(2,1)}), (bf16[256,8192]{1,0:T(8,128)(2,1)}, bf16[512,2048]{1,0:T(8,128)(2,1)})) %all-reduce.23.cloned.1.call-update) | async-done | bytes 6291472 | tf_op jit(solution)/shard_map/psum | solution.py:262
  (335 shorter events, 326.2 us)
Async XLA Ops:
  7.2 321.9 %copy-start = (bf16[8,12288]{1,0:T(8,128)(2,1)S(1)}, bf16[8,12288]{1,0:T(8,128)(2,1)}, u32[]{:S(2)}) copy-start(bf16[8,12288]{1,0:T(8,128)(2,1)} %param.24) | copy-start | bytes 589828
  7.3 166.2 %all-gather.3.cloned.1.call-start = ((), (), s32[]{:S(2)}) async-start(), calls=%async_computation.2 | async-start | bytes 37748736 | tf_op jit(solution)/shard_map/all_gather | solution.py:153
  8.0 257.3 %all-gather.5.cloned.1.call-start = ((), (), s32[]{:S(2)}) async-start(), calls=%async_computation.3 | async-start | bytes 18874368 | tf_op jit(solution)/shard_map/all_gather | solution.py:187
  8.8 3110.2 %reduce-scatter.5.cloned.1.call-start = ((), (), s32[]{:S(2)}) async-start(), calls=%async_computation.5 | async-start | bytes 18874368 | tf_op jit(solution)/shard_map/reduce_scatter | solution.py:253
  10.0 183.3 %copy-start.50 = (f32[2048]{0:T(1024)}, f32[2048]{0:T(1024)S(1)}, u32[]{:S(2)}) copy-start(f32[2048]{0:T(1024)S(1)} %convert_element_type.143) | copy-start | bytes 24580
  10.0 255.3 %copy-start.71 = (f32[4096]{0:T(1024)}, f32[4096]{0:T(1024)S(1)}, u32[]{:S(2)}) copy-start(f32[4096]{0:T(1024)S(1)} %convert_element_type.162) | copy-start | bytes 49156
  14.3 195.9 %copy-start.36 = (bf16[1,4,4,4,256]{2,3,4,1,0:T(4,128)(2,1)}, bf16[1,4,4,4,256]{2,3,4,1,0:T(4,128)(2,1)S(1)}, u32[]{:S(2)}) copy-start(bf16[1,4,4,4,256]{2,3,4,1,0:T(4,128)(2,1)S(1)} %copy.127) | copy-start | bytes 98308
  14.5 178.7 %copy-start.57 = (f32[256]{0:T(256)}, f32[256]{0:T(256)S(1)}, u32[]{:S(2)}) copy-start(f32[256]{0:T(256)S(1)} %broadcast_multiply_fusion.6) | copy-start | bytes 3076
  15.0 178.3 %copy-start.59 = (f32[256]{0:T(256)}, f32[256]{0:T(256)S(1)}, u32[]{:S(2)}) copy-start(f32[256]{0:T(256)S(1)} %fusion.114) | copy-start | bytes 3076
  15.4 177.9 %copy-start.46 = (bf16[256,2048]{1,0:T(8,128)(2,1)}, bf16[256,2048]{1,0:T(8,128)(2,1)S(1)}, u32[]{:S(2)}) copy-start(bf16[256,2048]{1,0:T(8,128)(2,1)S(1)} %fusion.57) | copy-start | bytes 3145732
  16.4 265.1 %copy-start.61 = (f32[1,4096]{1,0:T(1,128)}, f32[1,4096]{1,0:T(1,128)S(1)}, u32[]{:S(2)}) copy-start(f32[1,4096]{1,0:T(1,128)S(1)} %get-tuple-element.212) | copy-start | bytes 49156
  16.4 265.1 %copy-start.63 = (f32[1,4096]{1,0:T(1,128)}, f32[1,4096]{1,0:T(1,128)S(1)}, u32[]{:S(2)}) copy-start(f32[1,4096]{1,0:T(1,128)S(1)} %get-tuple-element.213) | copy-start | bytes 49156
  16.4 265.1 %copy-start.65 = (f32[1,4096]{1,0:T(1,128)}, f32[1,4096]{1,0:T(1,128)S(1)}, u32[]{:S(2)}) copy-start(f32[1,4096]{1,0:T(1,128)S(1)} %get-tuple-element.214) | copy-start | bytes 49156
  16.5 265.1 %copy-start.67 = (f32[1,4096]{1,0:T(1,128)}, f32[1,4096]{1,0:T(1,128)S(1)}, u32[]{:S(2)}) copy-start(f32[1,4096]{1,0:T(1,128)S(1)} %get-tuple-element.215) | copy-start | bytes 49156
  194.8 86.7 %collective-permute-start.2 = (bf16[3,4096]{1,0:T(4,128)(2,1)}, bf16[3,4096]{1,0:T(4,128)(2,1)S(1)}, u32[]{:S(2)}, u32[]{:S(2)}) collective-permute-start(bf16[3,4096]{1,0:T(4,128)(2,1)} %slice.91), channel_id=1, source_target_pairs={{0,1},{1,2},{2,3},{4,5},{5,6},{6,7},{8,9},{9,10},{10,11},{12,13},{... | collective-permute-start | bytes 73736 | tf_op jit(solution)/shard_map/ppermute | solution.py:14
  211.4 53.9 %copy-start.47 = (bf16[1,256,2048]{2,1,0:T(8,128)(2,1)S(1)}, bf16[1,256,2048]{2,1,0:T(8,128)(2,1)}, u32[]{:S(2)}) copy-start(bf16[1,256,2048]{2,1,0:T(8,128)(2,1)} %param.29) | copy-start | bytes 3145732
  211.4 53.9 %copy-start.86 = (f32[256]{0:T(256)S(1)}, f32[256]{0:T(256)}, u32[]{:S(2)}) copy-start(f32[256]{0:T(256)} %compare_convert_fusion) | copy-start | bytes 3076
  354.7 1214.6 %copy-start.45 = (bf16[4,256,256]{2,1,0:T(8,128)(2,1)}, bf16[4,256,256]{2,1,0:T(8,128)(2,1)S(1)}, u32[]{:S(2)}) copy-start(bf16[4,256,256]{2,1,0:T(8,128)(2,1)S(1)} %get-tuple-element.229) | copy-start | bytes 1572868
  355.0 32.1 copy-start.26
  412.4 363.6 %collective-permute-start = (f32[4,1024,1024]{2,1,0:T(8,128)}, f32[4,1024,1024]{2,1,0:T(8,128)}, u32[]{:S(2)}, u32[]{:S(2)}) collective-permute-start(f32[4,1024,1024]{2,1,0:T(8,128)} %multiply_add_fusion.10), channel_id=1, source_target_pairs={{0,1},{1,2},{2,3},{4,5},{5,6},{6,7},{8,9},{9,10},{10,11},{12,13},{... | collective-permute-start | bytes 50331656 | tf_op jit(solution)/shard_map/while/body/eval_jaxpr/ppermute | solution.py:14
  793.3 363.8 %collective-permute-start = (f32[4,1024,1024]{2,1,0:T(8,128)}, f32[4,1024,1024]{2,1,0:T(8,128)}, u32[]{:S(2)}, u32[]{:S(2)}) collective-permute-start(f32[4,1024,1024]{2,1,0:T(8,128)} %multiply_add_fusion.10), channel_id=1, source_target_pairs={{0,1},{1,2},{2,3},{4,5},{5,6},{6,7},{8,9},{9,10},{10,11},{12,13},{... | collective-permute-start | bytes 50331656 | tf_op jit(solution)/shard_map/while/body/eval_jaxpr/ppermute | solution.py:14
  1174.4 362.8 %collective-permute-start = (f32[4,1024,1024]{2,1,0:T(8,128)}, f32[4,1024,1024]{2,1,0:T(8,128)}, u32[]{:S(2)}, u32[]{:S(2)}) collective-permute-start(f32[4,1024,1024]{2,1,0:T(8,128)} %multiply_add_fusion.10), channel_id=1, source_target_pairs={{0,1},{1,2},{2,3},{4,5},{5,6},{6,7},{8,9},{9,10},{10,11},{12,13},{... | collective-permute-start | bytes 50331656 | tf_op jit(solution)/shard_map/while/body/eval_jaxpr/ppermute | solution.py:14
  1569.3 12.2 copy-start.17
  1587.7 25.6 copy-start.14
  1656.7 362.7 %collective-permute-start.1 = (f32[4,1024,1024]{2,1,0:T(8,128)}, f32[4,1024,1024]{2,1,0:T(8,128)}, u32[]{:S(2)}, u32[]{:S(2)}) collective-permute-start(f32[4,1024,1024]{2,1,0:T(8,128)} %multiply_add_fusion.11), channel_id=1, source_target_pairs={{1,0},{2,1},{3,2},{5,4},{6,5},{7,6},{9,8},{10,9},{11,10},{13,12},{... | collective-permute-start | bytes 50331656 | tf_op jit(solution)/shard_map/while/body/eval_jaxpr/ppermute | solution.py:14
  2036.7 361.3 %collective-permute-start.1 = (f32[4,1024,1024]{2,1,0:T(8,128)}, f32[4,1024,1024]{2,1,0:T(8,128)}, u32[]{:S(2)}, u32[]{:S(2)}) collective-permute-start(f32[4,1024,1024]{2,1,0:T(8,128)} %multiply_add_fusion.11), channel_id=1, source_target_pairs={{1,0},{2,1},{3,2},{5,4},{6,5},{7,6},{9,8},{10,9},{11,10},{13,12},{... | collective-permute-start | bytes 50331656 | tf_op jit(solution)/shard_map/while/body/eval_jaxpr/ppermute | solution.py:14
  2415.3 360.4 %collective-permute-start.1 = (f32[4,1024,1024]{2,1,0:T(8,128)}, f32[4,1024,1024]{2,1,0:T(8,128)}, u32[]{:S(2)}, u32[]{:S(2)}) collective-permute-start(f32[4,1024,1024]{2,1,0:T(8,128)} %multiply_add_fusion.11), channel_id=1, source_target_pairs={{1,0},{2,1},{3,2},{5,4},{6,5},{7,6},{9,8},{10,9},{11,10},{13,12},{... | collective-permute-start | bytes 50331656 | tf_op jit(solution)/shard_map/while/body/eval_jaxpr/ppermute | solution.py:14
  2775.7 12.8 copy-start.2
  2775.7 12.8 copy-start.27
  2775.7 12.9 copy-start.55
  2788.5 14.3 copy-start.12
  2865.3 11.6 copy-start.83
  2958.3 20.7 copy-start.48
  2958.3 20.6 copy-start.87
  2978.9 11.3 copy-start.34
  2990.2 323.6 %reduce-scatter.3.cloned.1.call-start = ((), (), s32[]{:S(2)}) async-start(), calls=%async_computation.4 | async-start | bytes 37748736 | tf_op jit(solution)/shard_map/reduce_scatter | solution.py:244
  3014.1 11.2 copy-start.22
  3023.8 22.4 collective-permute-start.3
  3069.9 413.6 %all-reduce.21.cloned.1.call-start = ((), (), s32[]{:S(2)}) async-start(), calls=%async_computation.6 | async-start | bytes 13500416 | tf_op jit(solution)/shard_map/psum | solution.py:265
  3088.7 17.5 copy-start.79
  3088.7 17.5 copy-start.81
  3106.8 11.2 copy-start.74
  3118.7 195.2 %copy-start.35 = (bf16[256,4096]{1,0:T(8,128)(2,1)S(1)}, bf16[256,4096]{1,0:T(8,128)(2,1)}, u32[]{:S(2)}) copy-start(bf16[256,4096]{1,0:T(8,128)(2,1)} %copy-done.34) | copy-start | bytes 6291460
  3118.7 195.2 %copy-start.88 = (f32[256]{0:T(256)S(1)}, f32[256]{0:T(256)}, u32[]{:S(2)}) copy-start(f32[256]{0:T(256)} %compare_convert_fusion) | copy-start | bytes 3076
  3118.7 590.2 %all-reduce.23.cloned.1.call-start = ((), (), s32[]{:S(2)}) async-start(), calls=%async_computation.7 | async-start | bytes 12582912 | tf_op jit(solution)/shard_map/psum | solution.py:262
  3314.0 12.7 copy-start.43
  3314.0 12.7 copy-start.44
  3326.7 15.3 copy-start.90
  (63 other events, 352.4 us)
Sparse Core Ops, SparseCore 0:
  10.0 163.4 all-gather.2
  175.4 89.8 all-gather.4
  2990.3 114.7 reduce-scatter.4
  3108.5 205.2 reduce-scatter.2
  3321.5 161.8 all-reduce.20
  3485.8 223.0 all-reduce.22
where the time goes:
time: 3730 us
  waiting for transfers between devices  2860 us (77%)
  matrix products  346 us (9%)
  other arithmetic  244 us (7%)
  local copies, waits for them, and re-layouts  180 us (5%)
  blocking collectives  41.4 us (1%)
  starting transfers between devices  38.6 us (1%)
    ppermute x8, waiting for transfers between devices, shifted(): return lax.ppermute(x, axis, pairs)  2140 us
    psum x1, waiting for transfers between devices, on_device(): lax.psum(up_part, 'ctx').astype(jnp.float32)  219 us
    reduce_scatter x1, waiting for transfers between devices, on_device(): lax.psum_scatter(lax.dot_general(columns, upward_grad, contract_first, pr...  195 us
    all_gather x1, waiting for transfers between devices, on_device(): lax.all_gather(up_weight, 'dp', axis=0, tiled=True)  157 us
    psum x1, waiting for transfers between devices, on_device(): lax.psum((norm_scale_grad, conv_taps_grad, conv_shift_grad, qkv_grad, gat...  95.7 us
  transfers between devices with their start and end apart: 14, of which 11 were waited for; matrix products, arithmetic and copies ran while one was open for 6% of the time, Pallas kernels for 0%

commit v1 on v0

--- a/solution.py
+++ b/solution.py
@@ -263,17 +263,20 @@
         lax.psum(down_part, "ctx").astype(jnp.float32),
     )
     small_total = lax.psum(
-        (
-            norm_scale_grad,
-            conv_taps_grad,
-            conv_shift_grad,
-            qkv_grad,
-            gate_matrix_grad,
-            gate_offset_grad,
-            skip_grad,
-            outnorm_grad,
+        lax.psum(
+            (
+                norm_scale_grad,
+                conv_taps_grad,
+                conv_shift_grad,
+                qkv_grad,
+                gate_matrix_grad,
+                gate_offset_grad,
+                skip_grad,
+                outnorm_grad,
+            ),
+            "ctx",
         ),
-        ("dp", "ctx"),
+        "dp",
     )
     return (
         outputs,

time: 3730 us -> 3970 us (1.064)
  waiting for transfers between devices: 2860 us -> 3100 us
    reduce_scatter x1, waiting for transfers between devices: 0.02 us -> 118 us  [on_device(): lax.psum_scatter(lax.dot_general(columns, branch_grad, contract_first, pr...]
    psum x1, waiting for transfers between devices: 95.7 us -> 163 us  [on_device(): lax.psum((norm_scale_grad, conv_taps_grad, conv_shift_grad, qkv_grad, gat...]
  transfers between devices with their start and end apart: 14 -> 15, of which waited for: 11 -> 13; matrix products, arithmetic and copies ran while one was open for 6% -> 4% of each run, Pallas kernels for 0% -> 0%
where the time goes in v1:
time: 3970 us; the launch traced here: 3960 us
  waiting for transfers between devices  3100 us (78%)
  matrix products  346 us (9%)
  other arithmetic  243 us (6%)
  local copies, waits for them, and re-layouts  178 us (4%)
  blocking collectives  43.7 us (1%)
    ppermute x8, waiting for transfers between devices, shifted(): return lax.ppermute(x, axis, pairs)  2140 us
    psum x1, waiting for transfers between devices, on_device(): lax.psum(up_part, 'ctx').astype(jnp.float32)  220 us
    reduce_scatter x1, waiting for transfers between devices, on_device(): lax.psum_scatter(lax.dot_general(columns, upward_grad, contract_first, pr...  209 us
    psum x1, waiting for transfers between devices, on_device(): lax.psum((norm_scale_grad, conv_taps_grad, conv_shift_grad, qkv_grad, gat...  163 us
    all_gather x1, waiting for transfers between devices, on_device(): lax.all_gather(up_weight, 'dp', axis=0, tiled=True)  157 us
    reduce_scatter x1, waiting for transfers between devices, on_device(): lax.psum_scatter(lax.dot_general(columns, branch_grad, contract_first, pr...  118 us
  transfers between devices with their start and end apart: 15, of which 13 were waited for; matrix products, arithmetic and copies ran while one was open for 4% of the time, Pallas kernels for 0%

profile of v1, /device:TPU:0, one launch (start us, length us, event | category | flops | bytes accessed | tf_op | source)
XLA Modules:
  0.0 3963.8 jit_solution(7765565035830504097)
XLA Ops:
  16.4 157.1 %all-gather.3.cloned.1.call-done = bf16[2048,8192]{1,0:T(8,128)(2,1)} async-done(((bf16[256,8192]{1,0:T(8,128)(2,1)}), bf16[2048,8192]{1,0:T(8,128)(2,1)}) %all-gather.3.cloned.1.call-update) | async-done | bytes 33554448 | tf_op jit(solution)/shard_map/all_gather | solution.py:153
  173.5 19.8 fusion.142
  214.1 51.2 %all-gather.5.cloned.1.call-done = bf16[4096,2048]{1,0:T(8,128)(2,1)} async-done(((bf16[512,2048]{1,0:T(8,128)(2,1)}), bf16[4096,2048]{1,0:T(8,128)(2,1)}) %all-gather.5.cloned.1.call-update) | async-done | bytes 16777232 | tf_op jit(solution)/shard_map/all_gather | solution.py:187
  265.3 12.4 broadcast_multiply_fusion
  344.2 10.2 fusion.100
  357.6 29.2 fusion.54
  394.8 1142.1 %while.24 = (s32[]{:T(128)}, f32[4,1024,1024]{2,1,0:T(8,128)}, f32[4,1,1]{0,2,1:T(1,128)S(1)}, f32[4,1024,1024]{2,1,0:T(8,128)}, s32[]{:T(128)}) while((s32[]{:T(128)}, f32[4,1024,1024]{2,1,0:T(8,128)}, f32[4,1,1]{0,2,1:T(1,128)S(1)}, f32[4,1024,1024]{2,1,0:T(8,128)}, s32[]{:T(128)}) %tuple.136), condition=%wide.region_5.6_spmd, body=%wide.region_4.5_spmd.sunk | while | flops 8388610 | bytes 117440624 | solution.py:170
  394.8 17.3 multiply_add_fusion.10
  412.1 9.2 collective-permute-start
  421.3 354.4 %collective-permute-done = f32[4,1024,1024]{2,1,0:T(8,128)} collective-permute-done((f32[4,1024,1024]{2,1,0:T(8,128)}, f32[4,1024,1024]{2,1,0:T(8,128)}, u32[]{:S(2)}, u32[]{:S(2)}) %collective-permute-start) | collective-permute-done | bytes 16777248 | tf_op jit(solution)/shard_map/while/body/eval_jaxpr/ppermute | solution.py:14
  775.7 17.3 multiply_add_fusion.10
  793.0 10.2 collective-permute-start
  803.2 353.6 %collective-permute-done = f32[4,1024,1024]{2,1,0:T(8,128)} collective-permute-done((f32[4,1024,1024]{2,1,0:T(8,128)}, f32[4,1024,1024]{2,1,0:T(8,128)}, u32[]{:S(2)}, u32[]{:S(2)}) %collective-permute-start) | collective-permute-done | bytes 16777248 | tf_op jit(solution)/shard_map/while/body/eval_jaxpr/ppermute | solution.py:14
  1156.8 17.3 multiply_add_fusion.10
  1174.1 10.2 collective-permute-start
  1184.3 352.7 %collective-permute-done = f32[4,1024,1024]{2,1,0:T(8,128)} collective-permute-done((f32[4,1024,1024]{2,1,0:T(8,128)}, f32[4,1024,1024]{2,1,0:T(8,128)}, u32[]{:S(2)}, u32[]{:S(2)}) %collective-permute-start) | collective-permute-done | bytes 16777248 | tf_op jit(solution)/shard_map/while/body/eval_jaxpr/ppermute | solution.py:14
  1536.9 9.3 convert_element_type.160
  1547.0 21.8 fusion.1
  1568.8 12.4 fusion.143
  1591.5 21.5 fusion
  1613.0 18.2 fusion.4
  1639.1 1136.3 %while.25 = (s32[]{:T(128)}, f32[4,1024,1024]{2,1,0:T(8,128)}, f32[4,1,1]{0,2,1:T(1,128)S(1)}, f32[4,1024,1024]{2,1,0:T(8,128)}, s32[]{:T(128)}) while((s32[]{:T(128)}, f32[4,1024,1024]{2,1,0:T(8,128)}, f32[4,1,1]{0,2,1:T(1,128)S(1)}, f32[4,1024,1024]{2,1,0:T(8,128)}, s32[]{:T(128)}) %tuple.137), condition=%wide.region_11.12_spmd, body=%wide.region_10.11_spmd.sunk | while | flops 8388610 | bytes 117440624 | solution.py:209
  1639.1 17.3 multiply_add_fusion.11
  1657.7 361.4 %collective-permute-done.1 = f32[4,1024,1024]{2,1,0:T(8,128)} collective-permute-done((f32[4,1024,1024]{2,1,0:T(8,128)}, f32[4,1024,1024]{2,1,0:T(8,128)}, u32[]{:S(2)}, u32[]{:S(2)}) %collective-permute-start.1) | collective-permute-done | bytes 16777248 | tf_op jit(solution)/shard_map/while/body/eval_jaxpr/ppermute | solution.py:14
  2019.1 17.3 multiply_add_fusion.11
  2037.7 360.0 %collective-permute-done.1 = f32[4,1024,1024]{2,1,0:T(8,128)} collective-permute-done((f32[4,1024,1024]{2,1,0:T(8,128)}, f32[4,1024,1024]{2,1,0:T(8,128)}, u32[]{:S(2)}, u32[]{:S(2)}) %collective-permute-start.1) | collective-permute-done | bytes 16777248 | tf_op jit(solution)/shard_map/while/body/eval_jaxpr/ppermute | solution.py:14
  2397.7 17.3 multiply_add_fusion.11
  2416.3 359.1 %collective-permute-done.1 = f32[4,1024,1024]{2,1,0:T(8,128)} collective-permute-done((f32[4,1024,1024]{2,1,0:T(8,128)}, f32[4,1024,1024]{2,1,0:T(8,128)}, u32[]{:S(2)}, u32[]{:S(2)}) %collective-permute-start.1) | collective-permute-done | bytes 16777248 | tf_op jit(solution)/shard_map/while/body/eval_jaxpr/ppermute | solution.py:14
  2775.4 12.8 multiply_reduce_fusion
  2788.2 14.1 fusion.39
  2802.4 18.7 fusion.36
  2832.7 15.5 fusion.2
  2848.3 8.1 fusion.107
  2891.3 13.5 fusion.17
  2918.1 10.9 fusion.84
  2948.9 10.9 fusion.87
  2995.3 20.3 multiply_reduce_fusion.1
  3041.6 10.5 convolution_convert_fusion.1
  3097.8 17.4 convolution_convert_fusion
  3115.3 163.1 %all-reduce.26.cloned.1.call-done = (f32[4,4096]{1,0:T(4,128)}, f32[3,4,4,4,256]{2,3,4,1,0:T(4,128)}, f32[8,12288]{1,0:T(8,128)}) async-done(((f32[4,4096]{1,0:T(4,128)}, f32[3,4,4,4,256]{2,3,4,1,0:T(4,128)}, f32[8,12288]{1,0:T(8,128)}), (f32[4,4096]{1,0:T(4,128)}, f32[3,4,4,4,256]{2,3,4,1,0:T(4,128)}, f32[8,12288]{1,0:T(8,128)})) %all-reduce.26.cloned.1.call-update) | async-done | bytes 655376 | tf_op jit(solution)/shard_map/psum | solution.py:266
  3278.6 118.4 %reduce-scatter.5.cloned.1.call-done = bf16[512,2048]{1,0:T(8,128)(2,1)} async-done(((bf16[4096,2048]{1,0:T(8,128)(2,1)}), bf16[512,2048]{1,0:T(8,128)(2,1)}) %reduce-scatter.5.cloned.1.call-update) | async-done | bytes 2097168 | tf_op jit(solution)/shard_map/reduce_scatter | solution.py:253
  3397.0 209.1 %reduce-scatter.3.cloned.1.call-done = bf16[256,8192]{1,0:T(8,128)(2,1)} async-done(((bf16[2048,8192]{1,0:T(8,128)(2,1)}), bf16[256,8192]{1,0:T(8,128)(2,1)}) %reduce-scatter.3.cloned.1.call-update) | async-done | bytes 4194320 | tf_op jit(solution)/shard_map/reduce_scatter | solution.py:244
  3606.3 12.7 fusion.53
  3619.0 15.0 fusion.71
  3635.0 19.7 all-reduce.17
  3654.7 24.0 all-reduce.15
  3682.1 38.0 all-reduce.24.cloned.1.call-done
  3726.2 219.7 %all-reduce.28.cloned.1.call-done = (bf16[256,8192]{1,0:T(8,128)(2,1)}, bf16[512,2048]{1,0:T(8,128)(2,1)}) async-done(((bf16[256,8192]{1,0:T(8,128)(2,1)}, bf16[512,2048]{1,0:T(8,128)(2,1)}), (bf16[256,8192]{1,0:T(8,128)(2,1)}, bf16[512,2048]{1,0:T(8,128)(2,1)})) %all-reduce.28.cloned.1.call-update) | async-done | bytes 6291472 | tf_op jit(solution)/shard_map/psum | solution.py:262
  (331 shorter events, 337.6 us)
Async XLA Ops:
  7.2 321.8 %copy-start = (bf16[8,12288]{1,0:T(8,128)(2,1)S(1)}, bf16[8,12288]{1,0:T(8,128)(2,1)}, u32[]{:S(2)}) copy-start(bf16[8,12288]{1,0:T(8,128)(2,1)} %param.24) | copy-start | bytes 589828
  7.3 166.2 %all-gather.3.cloned.1.call-start = ((), (), s32[]{:S(2)}) async-start(), calls=%async_computation.2 | async-start | bytes 37748736 | tf_op jit(solution)/shard_map/all_gather | solution.py:153
  8.0 257.3 %all-gather.5.cloned.1.call-start = ((), (), s32[]{:S(2)}) async-start(), calls=%async_computation.3 | async-start | bytes 18874368 | tf_op jit(solution)/shard_map/all_gather | solution.py:187
  8.8 3269.5 %all-reduce.26.cloned.1.call-start = ((), (), s32[]{:S(2)}) async-start(), calls=%async_computation.7 | async-start | bytes 13500416 | tf_op jit(solution)/shard_map/psum | solution.py:266
  10.0 183.3 %copy-start.52 = (f32[2048]{0:T(1024)}, f32[2048]{0:T(1024)S(1)}, u32[]{:S(2)}) copy-start(f32[2048]{0:T(1024)S(1)} %convert_element_type.143) | copy-start | bytes 24580
  10.0 255.3 %copy-start.73 = (f32[4096]{0:T(1024)}, f32[4096]{0:T(1024)S(1)}, u32[]{:S(2)}) copy-start(f32[4096]{0:T(1024)S(1)} %convert_element_type.162) | copy-start | bytes 49156
  14.3 195.7 %copy-start.35 = (bf16[1,4,4,4,256]{2,3,4,1,0:T(4,128)(2,1)}, bf16[1,4,4,4,256]{2,3,4,1,0:T(4,128)(2,1)S(1)}, u32[]{:S(2)}) copy-start(bf16[1,4,4,4,256]{2,3,4,1,0:T(4,128)(2,1)S(1)} %copy.127) | copy-start | bytes 98308
  14.5 178.8 %copy-start.59 = (f32[256]{0:T(256)}, f32[256]{0:T(256)S(1)}, u32[]{:S(2)}) copy-start(f32[256]{0:T(256)S(1)} %broadcast_multiply_fusion.6) | copy-start | bytes 3076
  15.0 178.3 %copy-start.61 = (f32[256]{0:T(256)}, f32[256]{0:T(256)S(1)}, u32[]{:S(2)}) copy-start(f32[256]{0:T(256)S(1)} %fusion.114) | copy-start | bytes 3076
  15.4 177.9 %copy-start.48 = (bf16[256,2048]{1,0:T(8,128)(2,1)}, bf16[256,2048]{1,0:T(8,128)(2,1)S(1)}, u32[]{:S(2)}) copy-start(bf16[256,2048]{1,0:T(8,128)(2,1)S(1)} %fusion.57) | copy-start | bytes 3145732
  16.4 265.2 %copy-start.63 = (f32[1,4096]{1,0:T(1,128)}, f32[1,4096]{1,0:T(1,128)S(1)}, u32[]{:S(2)}) copy-start(f32[1,4096]{1,0:T(1,128)S(1)} %get-tuple-element.220) | copy-start | bytes 49156
  16.4 265.2 %copy-start.65 = (f32[1,4096]{1,0:T(1,128)}, f32[1,4096]{1,0:T(1,128)S(1)}, u32[]{:S(2)}) copy-start(f32[1,4096]{1,0:T(1,128)S(1)} %get-tuple-element.221) | copy-start | bytes 49156
  16.4 265.2 %copy-start.67 = (f32[1,4096]{1,0:T(1,128)}, f32[1,4096]{1,0:T(1,128)S(1)}, u32[]{:S(2)}) copy-start(f32[1,4096]{1,0:T(1,128)S(1)} %get-tuple-element.222) | copy-start | bytes 49156
  16.4 265.2 %copy-start.69 = (f32[1,4096]{1,0:T(1,128)}, f32[1,4096]{1,0:T(1,128)S(1)}, u32[]{:S(2)}) copy-start(f32[1,4096]{1,0:T(1,128)S(1)} %get-tuple-element.223) | copy-start | bytes 49156
  194.8 86.7 %collective-permute-start.2 = (bf16[3,4096]{1,0:T(4,128)(2,1)}, bf16[3,4096]{1,0:T(4,128)(2,1)S(1)}, u32[]{:S(2)}, u32[]{:S(2)}) collective-permute-start(bf16[3,4096]{1,0:T(4,128)(2,1)} %slice.91), channel_id=1, source_target_pairs={{0,1},{1,2},{2,3},{4,5},{5,6},{6,7},{8,9},{9,10},{10,11},{12,13},{... | collective-permute-start | bytes 73736 | tf_op jit(solution)/shard_map/ppermute | solution.py:14
  211.3 54.0 %copy-start.49 = (bf16[1,256,2048]{2,1,0:T(8,128)(2,1)S(1)}, bf16[1,256,2048]{2,1,0:T(8,128)(2,1)}, u32[]{:S(2)}) copy-start(bf16[1,256,2048]{2,1,0:T(8,128)(2,1)} %param.29) | copy-start | bytes 3145732
  211.3 54.0 %copy-start.83 = (f32[256]{0:T(256)S(1)}, f32[256]{0:T(256)}, u32[]{:S(2)}) copy-start(f32[256]{0:T(256)} %compare_convert_fusion) | copy-start | bytes 3076
  344.2 10.6 copy-start.56
  354.5 1214.3 %copy-start.46 = (bf16[4,256,256]{2,1,0:T(8,128)(2,1)}, bf16[4,256,256]{2,1,0:T(8,128)(2,1)S(1)}, u32[]{:S(2)}) copy-start(bf16[4,256,256]{2,1,0:T(8,128)(2,1)S(1)} %get-tuple-element.237) | copy-start | bytes 1572868
  354.8 32.1 copy-start.24
  412.1 363.6 %collective-permute-start = (f32[4,1024,1024]{2,1,0:T(8,128)}, f32[4,1024,1024]{2,1,0:T(8,128)}, u32[]{:S(2)}, u32[]{:S(2)}) collective-permute-start(f32[4,1024,1024]{2,1,0:T(8,128)} %multiply_add_fusion.10), channel_id=1, source_target_pairs={{0,1},{1,2},{2,3},{4,5},{5,6},{6,7},{8,9},{9,10},{10,11},{12,13},{... | collective-permute-start | bytes 50331656 | tf_op jit(solution)/shard_map/while/body/eval_jaxpr/ppermute | solution.py:14
  793.0 363.8 %collective-permute-start = (f32[4,1024,1024]{2,1,0:T(8,128)}, f32[4,1024,1024]{2,1,0:T(8,128)}, u32[]{:S(2)}, u32[]{:S(2)}) collective-permute-start(f32[4,1024,1024]{2,1,0:T(8,128)} %multiply_add_fusion.10), channel_id=1, source_target_pairs={{0,1},{1,2},{2,3},{4,5},{5,6},{6,7},{8,9},{9,10},{10,11},{12,13},{... | collective-permute-start | bytes 50331656 | tf_op jit(solution)/shard_map/while/body/eval_jaxpr/ppermute | solution.py:14
  1174.1 362.9 %collective-permute-start = (f32[4,1024,1024]{2,1,0:T(8,128)}, f32[4,1024,1024]{2,1,0:T(8,128)}, u32[]{:S(2)}, u32[]{:S(2)}) collective-permute-start(f32[4,1024,1024]{2,1,0:T(8,128)} %multiply_add_fusion.10), channel_id=1, source_target_pairs={{0,1},{1,2},{2,3},{4,5},{5,6},{6,7},{8,9},{9,10},{10,11},{12,13},{... | collective-permute-start | bytes 50331656 | tf_op jit(solution)/shard_map/while/body/eval_jaxpr/ppermute | solution.py:14
  1568.8 12.4 copy-start.15
  1587.4 25.6 copy-start.12
  1656.4 362.7 %collective-permute-start.1 = (f32[4,1024,1024]{2,1,0:T(8,128)}, f32[4,1024,1024]{2,1,0:T(8,128)}, u32[]{:S(2)}, u32[]{:S(2)}) collective-permute-start(f32[4,1024,1024]{2,1,0:T(8,128)} %multiply_add_fusion.11), channel_id=1, source_target_pairs={{1,0},{2,1},{3,2},{5,4},{6,5},{7,6},{9,8},{10,9},{11,10},{13,12},{... | collective-permute-start | bytes 50331656 | tf_op jit(solution)/shard_map/while/body/eval_jaxpr/ppermute | solution.py:14
  2036.4 361.3 %collective-permute-start.1 = (f32[4,1024,1024]{2,1,0:T(8,128)}, f32[4,1024,1024]{2,1,0:T(8,128)}, u32[]{:S(2)}, u32[]{:S(2)}) collective-permute-start(f32[4,1024,1024]{2,1,0:T(8,128)} %multiply_add_fusion.11), channel_id=1, source_target_pairs={{1,0},{2,1},{3,2},{5,4},{6,5},{7,6},{9,8},{10,9},{11,10},{13,12},{... | collective-permute-start | bytes 50331656 | tf_op jit(solution)/shard_map/while/body/eval_jaxpr/ppermute | solution.py:14
  2415.0 360.4 %collective-permute-start.1 = (f32[4,1024,1024]{2,1,0:T(8,128)}, f32[4,1024,1024]{2,1,0:T(8,128)}, u32[]{:S(2)}, u32[]{:S(2)}) collective-permute-start(f32[4,1024,1024]{2,1,0:T(8,128)} %multiply_add_fusion.11), channel_id=1, source_target_pairs={{1,0},{2,1},{3,2},{5,4},{6,5},{7,6},{9,8},{10,9},{11,10},{13,12},{... | collective-permute-start | bytes 50331656 | tf_op jit(solution)/shard_map/while/body/eval_jaxpr/ppermute | solution.py:14
  2775.4 12.8 copy-start.2
  2775.4 12.8 copy-start.25
  2775.4 12.9 copy-start.57
  2788.2 14.1 copy-start.11
  2802.3 18.7 copy-start.78
  2802.3 18.7 copy-start.82
  2802.3 30.4 copy-start.80
  2918.1 10.9 copy-start.20
  2918.1 10.9 copy-start.39
  2948.9 10.9 copy-start.19
  2948.9 10.9 copy-start.37
  3040.4 356.6 %reduce-scatter.5.cloned.1.call-start = ((), (), s32[]{:S(2)}) async-start(), calls=%async_computation.5 | async-start | bytes 18874368 | tf_op jit(solution)/shard_map/reduce_scatter | solution.py:253
  3052.1 554.1 %reduce-scatter.3.cloned.1.call-start = ((), (), s32[]{:S(2)}) async-start(), calls=%async_computation.4 | async-start | bytes 37748736 | tf_op jit(solution)/shard_map/reduce_scatter | solution.py:244
  3069.8 22.2 collective-permute-start.3
  3115.2 604.9 %all-reduce.24.cloned.1.call-start = ((), (), s32[]{:S(2)}) async-start(), calls=%async_computation.6 | async-start | bytes 13500416 | tf_op jit(solution)/shard_map/psum | solution.py:265
  3278.3 328.0 %copy-start.34 = (bf16[256,4096]{1,0:T(8,128)(2,1)S(1)}, bf16[256,4096]{1,0:T(8,128)(2,1)}, u32[]{:S(2)}) copy-start(bf16[256,4096]{1,0:T(8,128)(2,1)} %get-tuple-element.207) | copy-start | bytes 6291460
  3278.3 667.5 %all-reduce.28.cloned.1.call-start = ((), (), s32[]{:S(2)}) async-start(), calls=%async_computation.8 | async-start | bytes 12582912 | tf_op jit(solution)/shard_map/psum | solution.py:262
  3606.3 12.7 copy-start.42
  3606.3 12.7 copy-start.43
  3619.0 15.0 copy-start.86
  (60 other events, 287.8 us)
Sparse Core Ops, SparseCore 0:
  10.0 163.4 all-gather.2
  175.4 89.8 all-gather.4
  3040.5 237.7 all-reduce.25
  3282.1 114.8 reduce-scatter.4
  3400.8 205.2 reduce-scatter.2
  3609.6 110.4 all-reduce.23
  3722.5 223.2 all-reduce.27
